TPU v7x, 32 devices: a whole 2x2x4 slice. The times are simulated.
32 devices in a mesh: expert: 8 (over y, x, core), tensor: 4 (over z).
Axes of the slice: x: 2, y: 2, z: 4, core: 2. Of those that a mesh axis runs over, the one named last changes fastest.
Arguments:
- inputs: float32 [7880, 512], P('expert'), may hold values from -6 to 6
- cotangent: float32 [7880, 512], P('expert'), may hold values from -6 to 6
- routes: int32 [2, 7880, 2], P(None, 'expert'), may hold values from 0 to 7, all different within a row
- priority: int32 [2, 7880], P(None, 'expert'), may hold values from 0 to 984, as said below
- attend_in: float32 [2, 3, 512, 512], P(None, None, 'expert', 'tensor'), may hold values from -0.375 to 0.375
- attend_out: float32 [2, 512, 512], P(None, 'tensor', 'expert'), may hold values from -1.5 to 1.5
- router: float32 [2, 512, 8], P(None, None, 'expert'), may hold values from -0.1875 to 0.1875
- norm_gains: float32 [2, 2, 512], P(None, None, 'expert'), may hold values from 0.25 to 1.75
- expert_in: float32 [2, 8, 512, 2048], P(None, 'expert', None, 'tensor'), may hold values from -0.25 to 0.25
- expert_out: float32 [2, 8, 2048, 512], P(None, 'expert', 'tensor'), may hold values from -0.5 to 0.5
Outputs:
- outputs: float32 [7880, 512], P('expert')
- input_grad: float32 [7880, 512], P('expert')
- attend_in_grad: float32 [2, 3, 512, 512], P(None, None, 'expert', 'tensor')
- attend_out_grad: float32 [2, 512, 512], P(None, 'tensor', 'expert')
- router_grad: float32 [2, 512, 8], P(None, None, 'expert')
- gains_grad: float32 [2, 2, 512], P(None, None, 'expert')
- expert_in_grad: float32 [2, 8, 512, 2048], P(None, 'expert', None, 'tensor')
- expert_out_grad: float32 [2, 8, 2048, 512], P(None, 'expert', 'tensor')
Inputs may be any that keep to these rules, and one draw needn't show every extreme that they name: `routes`: in each block each token names two different experts, and every expert is named by some token. `priority`: in each block, the values within each device's 985 tokens are a permutation.
All inputs are finite; a program needn't handle non-finite values.
Results may differ from a plain program's by a relative error of at most 0.025.
The roundings to bfloat16 on the way count: a program that leaves them out, or rounds other values in their place, can miss the bound.
Values may be sent and summed in bfloat16 or wider, within the bound.
A program may use at most 192 MiB of HBM per device.

v0:
```python
import jax
import jax.numpy as jnp
from jax import lax
from jax.sharding import PartitionSpec as P

HEAD_DIM = 64
SEQ = 197


def norm_rows(rows_in, gain_row):
    centred = rows_in - jnp.mean(rows_in, axis=-1, keepdims=True)
    spread = jnp.mean(centred * centred, axis=-1, keepdims=True)
    return centred * lax.rsqrt(spread + 1e-06) * gain_row


def gelu_exact(rows_in):
    return 0.5 * rows_in * (1.0 + lax.erf(rows_in * 0.7071067811865476))


def contract_rows(left_side, right_side):
    return lax.dot_general(
        left_side, right_side, (((0,), (0,)), ((), ())), preferred_element_type=jnp.float32
    )


def contract_last(left_side, right_side):
    return lax.dot_general(
        left_side, right_side, (((1,), (1,)), ((), ())), preferred_element_type=jnp.float32
    )


def exchange(rows):
    return lax.all_to_all(rows, "expert", split_axis=0, concat_axis=0, tiled=True)


def own_part(rows, width, axis=1):
    return lax.dynamic_slice_in_dim(rows, lax.axis_index("tensor") * width, width, axis=axis)


def slot_plan(chosen, rank_rows, experts, capacity):
    columns = lax.broadcasted_iota(jnp.int32, (1, experts), 1)
    first_hot = (chosen[:, 0:1] == columns).astype(jnp.bfloat16)
    second = (chosen[:, 1:2] == columns).astype(jnp.bfloat16)
    earlier = (rank_rows[None, :] < rank_rows[:, None]).astype(jnp.bfloat16)
    count_first = jnp.dot(earlier, first_hot, preferred_element_type=jnp.float32)
    count_second = jnp.dot(earlier, second, preferred_element_type=jnp.float32)
    first_f = first_hot.astype(jnp.float32)
    second_f = second.astype(jnp.float32)
    filled = jnp.sum(first_f, axis=0, keepdims=True)
    slot_first = jnp.sum(count_first * first_f, axis=1)
    slot_second = jnp.sum((filled + count_second) * second_f, axis=1)
    slot_nums = jnp.stack([slot_first, slot_second], axis=1).astype(jnp.int32)
    target = jnp.where(slot_nums < capacity, chosen * capacity + slot_nums, experts * capacity)
    return (target, first_f, second_f)


def local(
    inputs,
    cotangent,
    routes,
    priority,
    attend_in,
    attend_out,
    router,
    norm_gains,
    expert_in,
    expert_out,
):
    experts = lax.axis_size("expert")
    tokens = inputs.shape[0]
    model_width = inputs.shape[1]
    images = tokens // SEQ
    head_cols = attend_in.shape[3]
    hidden_cols = expert_in.shape[3]
    local_heads = head_cols * lax.axis_size("tensor") // HEAD_DIM
    layers = attend_in.shape[0]
    capacity = max(2, (10 * tokens + 4 * experts - 1) // (4 * experts))
    slots_all = experts * capacity
    score_scale = HEAD_DIM ** (-0.5)
    layer_ids = range(layers)
    gains_full = lax.all_gather(norm_gains.astype(jnp.bfloat16), "expert", axis=2, tiled=True)
    router_full = lax.all_gather(router.astype(jnp.bfloat16), "expert", axis=2, tiled=True)
    in_full = []
    out_full = []
    win_full = []
    wout_full = []
    for layer_index in layer_ids:
        in_part = lax.all_gather(
            attend_in[layer_index].astype(jnp.bfloat16), "tensor", axis=2, tiled=True
        )
        in_full.append(lax.all_gather(in_part, "expert", axis=1, tiled=True))
        out_part = lax.all_gather(
            attend_out[layer_index].astype(jnp.bfloat16), "tensor", axis=0, tiled=True
        )
        out_full.append(lax.all_gather(out_part, "expert", axis=1, tiled=True))
        win_full.append(
            lax.all_gather(
                expert_in[layer_index, 0].astype(jnp.bfloat16), "tensor", axis=1, tiled=True
            )
        )
        wout_full.append(
            lax.all_gather(
                expert_out[layer_index, 0].astype(jnp.bfloat16), "tensor", axis=0, tiled=True
            )
        )
    slot_ids = lax.broadcasted_iota(jnp.int32, (1, slots_all), 1)
    stream = inputs
    stash_list = []
    for layer_index in range(layers):
        gains_now = gains_full[layer_index].astype(jnp.float32)
        normed = norm_rows(stream, gains_now[0]).astype(jnp.bfloat16)
        project = in_full[layer_index]
        triple = jnp.einsum(
            "td,jdh->jth", normed, project, preferred_element_type=jnp.float32
        ).astype(jnp.bfloat16)
        shaped = triple.reshape(3, images, SEQ, local_heads, HEAD_DIM)
        scores = (
            jnp.einsum("iqhd,ikhd->ihqk", shaped[0], shaped[1], preferred_element_type=jnp.float32)
            * score_scale
        )
        log_total = jax.nn.logsumexp(scores, axis=-1, keepdims=True)
        attention = jnp.exp(scores - log_total).astype(jnp.bfloat16)
        mixed_heads = (
            jnp.einsum("ihqk,ikhd->iqhd", attention, shaped[2], preferred_element_type=jnp.float32)
            .astype(jnp.bfloat16)
            .reshape(tokens, -1)
        )
        middle = stream + jnp.dot(
            mixed_heads, out_full[layer_index], preferred_element_type=jnp.float32
        )
        normed_two = norm_rows(middle, gains_now[1]).astype(jnp.bfloat16)
        logits = jnp.dot(normed_two, router_full[layer_index], preferred_element_type=jnp.float32)
        probs_all = jax.nn.softmax(logits, axis=-1)
        chosen = routes[layer_index]
        target, first_f, second_f = slot_plan(chosen, priority[layer_index], experts, capacity)
        gate_values = jnp.stack(
            [jnp.sum(probs_all * first_f, axis=1), jnp.sum(probs_all * second_f, axis=1)], axis=1
        )
        pick_first = (target[:, 0:1] == slot_ids).astype(jnp.bfloat16)
        pick_second = (target[:, 1:2] == slot_ids).astype(jnp.bfloat16)
        pick_both = pick_first + pick_second
        dispatched = contract_rows(pick_both, normed_two).astype(jnp.bfloat16)
        arrived = exchange(dispatched.reshape(experts, capacity, model_width)).reshape(
            slots_all, model_width
        )
        before = jnp.dot(arrived, win_full[layer_index], preferred_element_type=jnp.float32)
        hidden = gelu_exact(before).astype(jnp.bfloat16)
        expert_rows = jnp.dot(
            hidden, wout_full[layer_index], preferred_element_type=jnp.float32
        ).astype(jnp.bfloat16)
        returned = exchange(expert_rows.reshape(experts, capacity, model_width)).reshape(
            slots_all, model_width
        )
        rows_first = jnp.dot(pick_first, returned, preferred_element_type=jnp.float32)
        rows_second = jnp.dot(pick_second, returned, preferred_element_type=jnp.float32)
        output = middle + gate_values[:, 0:1] * rows_first + gate_values[:, 1:2] * rows_second
        stash_list.append(
            (
                stream,
                gains_now,
                normed,
                shaped,
                log_total,
                mixed_heads,
                middle,
                normed_two,
                probs_all,
                gate_values,
                target,
                first_f,
                second_f,
                pick_first,
                pick_second,
                pick_both,
                arrived,
                rows_first,
                rows_second,
            )
        )
        stream = output
    upstream = cotangent
    grads_in, grads_out, grads_router, grads_gain, grads_win, grads_wout = ([], [], [], [], [], [])
    for layer_index in reversed(range(layers)):
        (
            stream_in,
            gains_now,
            normed,
            shaped,
            log_total,
            mixed_heads,
            middle,
            normed_two,
            probs_all,
            gate_values,
            target,
            first_f,
            second_f,
            pick_first,
            pick_second,
            pick_both,
            arrived,
            rows_first,
            rows_second,
        ) = stash_list[layer_index]
        gate_first = jnp.sum(upstream * rows_first, axis=1)
        gate_second = jnp.sum(upstream * rows_second, axis=1)
        scaled_first = (gate_values[:, 0:1] * upstream).astype(jnp.bfloat16)
        scaled_second = (gate_values[:, 1:2] * upstream).astype(jnp.bfloat16)
        grad_slots = (
            contract_rows(pick_first, scaled_first) + contract_rows(pick_second, scaled_second)
        ).astype(jnp.bfloat16)
        grad_arrived = exchange(grad_slots.reshape(experts, capacity, model_width)).reshape(
            slots_all, model_width
        )
        before = jnp.dot(arrived, win_full[layer_index], preferred_element_type=jnp.float32)
        hidden = gelu_exact(before).astype(jnp.bfloat16)
        grads_wout.append(contract_rows(own_part(hidden, hidden_cols), grad_arrived))
        grad_hidden = contract_last(grad_arrived, wout_full[layer_index])
        grad_before = jax.vjp(gelu_exact, before)[1](grad_hidden)[0].astype(jnp.bfloat16)
        grads_win.append(contract_rows(arrived, own_part(grad_before, hidden_cols)))
        grad_rows = contract_last(grad_before, win_full[layer_index]).astype(jnp.bfloat16)
        grad_dispatched = exchange(grad_rows.reshape(experts, capacity, model_width)).reshape(
            slots_all, model_width
        )
        grad_normed = jnp.dot(pick_both, grad_dispatched, preferred_element_type=jnp.float32)
        grad_probs = first_f * gate_first[:, None] + second_f * gate_second[:, None]
        grad_logits = (
            probs_all * (grad_probs - jnp.sum(probs_all * grad_probs, axis=1, keepdims=True))
        ).astype(jnp.bfloat16)
        grads_router.append(contract_rows(normed_two, grad_logits))
        grad_normed = grad_normed + contract_last(grad_logits, router_full[layer_index])
        norm_back = jax.vjp(norm_rows, middle, gains_now[1])[1](grad_normed)
        grad_middle = upstream + norm_back[0]
        grad_branch = grad_middle.astype(jnp.bfloat16)
        grads_out.append(contract_rows(own_part(mixed_heads, head_cols), grad_branch))
        grad_mixed = (
            contract_last(grad_branch, out_full[layer_index])
            .astype(jnp.bfloat16)
            .reshape(images, SEQ, local_heads, HEAD_DIM)
        )
        scores = (
            jnp.einsum("iqhd,ikhd->ihqk", shaped[0], shaped[1], preferred_element_type=jnp.float32)
            * score_scale
        )
        attention_f = jnp.exp(scores - log_total)
        attention = attention_f.astype(jnp.bfloat16)
        grad_value = jnp.einsum(
            "ihqk,iqhd->ikhd", attention, grad_mixed, preferred_element_type=jnp.float32
        ).astype(jnp.bfloat16)
        grad_attention = jnp.einsum(
            "iqhd,ikhd->ihqk", grad_mixed, shaped[2], preferred_element_type=jnp.float32
        )
        grad_scores = (
            attention_f
            * (grad_attention - jnp.sum(attention_f * grad_attention, axis=-1, keepdims=True))
        ).astype(jnp.bfloat16)
        grad_query = (
            jnp.einsum(
                "ihqk,ikhd->iqhd", grad_scores, shaped[1], preferred_element_type=jnp.float32
            )
            * score_scale
        ).astype(jnp.bfloat16)
        grad_key = (
            jnp.einsum(
                "ihqk,iqhd->ikhd", grad_scores, shaped[0], preferred_element_type=jnp.float32
            )
            * score_scale
        ).astype(jnp.bfloat16)
        grad_triple = jnp.stack([grad_query, grad_key, grad_value]).reshape(3, tokens, -1)
        grads_in.append(
            jnp.einsum(
                "td,jth->jdh",
                normed,
                own_part(grad_triple, head_cols, 2),
                preferred_element_type=jnp.float32,
            )
        )
        project = in_full[layer_index]
        grad_normed_one = jnp.einsum(
            "jth,jdh->td", grad_triple, project, preferred_element_type=jnp.float32
        )
        norm_back_one = jax.vjp(norm_rows, stream_in, gains_now[0])[1](grad_normed_one)
        grads_gain.append(jnp.stack([norm_back_one[1], norm_back[1]]))
        upstream = grad_middle + norm_back_one[0]
    in_grad_all = jnp.stack(grads_in[::-1])
    out_grad_all = jnp.stack(grads_out[::-1])
    router_grad_all = jnp.stack(grads_router[::-1])
    gain_grad_all = jnp.stack(grads_gain[::-1])
    reduced = (
        lax.psum_scatter(in_grad_all, "expert", scatter_dimension=2, tiled=True),
        lax.psum_scatter(out_grad_all, "expert", scatter_dimension=2, tiled=True),
        lax.psum_scatter(router_grad_all, "expert", scatter_dimension=2, tiled=True),
        lax.psum_scatter(gain_grad_all, "expert", scatter_dimension=2, tiled=True),
    )
    win_grad_all = jnp.stack(grads_win[::-1])[:, None]
    wout_grad_all = jnp.stack(grads_wout[::-1])[:, None]
    return (
        stream,
        upstream,
        reduced[0],
        reduced[1],
        reduced[2],
        reduced[3],
        win_grad_all,
        wout_grad_all,
    )


def solution(mesh):
    placed = (
        P("expert", None),
        P("expert", None),
        P(None, "expert", None),
        P(None, "expert"),
        P(None, None, "expert", "tensor"),
        P(None, "tensor", "expert"),
        P(None, None, "expert"),
        P(None, None, "expert"),
        P(None, "expert", None, "tensor"),
        P(None, "expert", "tensor", None),
    )
    return jax.shard_map(
        local,
        mesh=mesh,
        in_specs=placed,
        out_specs=(
            P("expert", None),
            P("expert", None),
            P(None, None, "expert", "tensor"),
            P(None, "tensor", "expert"),
            P(None, None, "expert"),
            P(None, None, "expert"),
            P(None, "expert", None, "tensor"),
            P(None, "expert", "tensor", None),
        ),
        check_vma=False,
    )
```

profile of v0, /device:TPU:0, one launch (start us, length us, event | category | flops | bytes accessed | tf_op | source)
XLA Modules:
  0.0 926.4 jit_solution(8189973012302681919)
XLA Ops:
  8.2 14.9 %all-gather = bf16[1,3,64,512]{3,2,1,0:T(8,128)(2,1)} all-gather(bf16[1,3,64,128]{3,2,1,0:T(8,128)(2,1)S(1)} %get-tuple-element.97), channel_id=2, replica_groups=mesh['expert'=8,'tensor'=4] {'tensor'}, dimensions={3}, use_global_device_ids=true | all-gather | bytes 245760 | tf_op jit(solution)/shard_map/all_gather | solution.py:88
  30.4 9.6 %all_gather.42 = bf16[2,2,512]{1,0,2:T(2,128)(2,1)S(1)} all-gather(bf16[2,2,64]{1,0,2:T(2,128)(2,1)S(1)} %copy.168), channel_id=1, replica_groups=mesh['expert'=8,'tensor'=4] {'expert'}, dimensions={2}, use_global_device_ids=true | all-gather | bytes 4608 | tf_op jit(solution)/shard_map/all_gather | solution.py:81
  43.8 12.0 %all-gather.2 = bf16[1,512,64]{1,2,0:T(8,128)(2,1)S(1)} all-gather(bf16[1,128,64]{1,2,0:T(8,128)(2,1)S(1)} %get-tuple-element.99), channel_id=4, replica_groups=mesh['expert'=8,'tensor'=4] {'tensor'}, dimensions={1}, use_global_device_ids=true | all-gather | bytes 81920 | tf_op jit(solution)/shard_map/all_gather | solution.py:92
  55.8 10.5 %all-gather.3 = bf16[1,512,512]{1,2,0:T(8,128)(2,1)} all-gather(bf16[1,512,64]{1,2,0:T(8,128)(2,1)S(1)} %all-gather.2), channel_id=5, replica_groups=mesh['expert'=8,'tensor'=4] {'expert'}, dimensions={2}, use_global_device_ids=true | all-gather | bytes 589824 | tf_op jit(solution)/shard_map/all_gather | solution.py:95
  66.3 8.2 all_gather.47
  107.4 6.5 fusion.98
  137.0 14.4 %all-gather.6 = bf16[1,3,64,512]{3,2,1,0:T(8,128)(2,1)} all-gather(bf16[1,3,64,128]{3,2,1,0:T(8,128)(2,1)S(1)} %get-tuple-element.96), channel_id=8, replica_groups=mesh['expert'=8,'tensor'=4] {'tensor'}, dimensions={3}, use_global_device_ids=true | all-gather | bytes 245760 | tf_op jit(solution)/shard_map/all_gather | solution.py:88
  151.4 19.1 %all-to-all-done = bf16[8,308,512]{2,1,0:T(8,128)(2,1)S(1)} async-done(((bf16[8,308,512]{2,1,0:T(8,128)(2,1)}), bf16[8,308,512]{2,1,0:T(8,128)(2,1)S(1)}, u32[]{:S(2)}, u32[]{:S(2)}) %all-to-all-start) | async-done | bytes 2523168 | tf_op jit(solution)/shard_map/all_to_all | solution.py:33
  172.7 13.4 %multiply_convert_fusion.1 = (bf16[2464,2048]{1,0:T(8,128)(2,1)}, f32[2464,2048]{1,0:T(8,128)}) fusion(bf16[2464,512]{1,0:T(8,128)(2,1)} %reshape.292, bf16[1,1,512,2048]{3,2,1,0:T(8,128)(2,1)} %all-gather.21.cloned.1.call-done), kind=kOutput, calls=%fused_computation.4 | convolution fusion | flops 5192613888 | bytes 34897920 | tf_op jit(solution)/shard_map/dot_general | solution.py:146
  186.1 9.8 %convolution_convert_fusion.3 = bf16[2464,512]{1,0:T(8,128)(2,1)S(1)} fusion(bf16[2464,2048]{1,0:T(8,128)(2,1)} %get-tuple-element.122, bf16[1,1,2048,512]{3,2,1,0:T(8,128)(2,1)} %all-gather.23.cloned.1.call-done), kind=kOutput, calls=%fused_computation.71 | convolution fusion | flops 5168644096 | bytes 14712832 | tf_op jit(solution)/shard_map/dot_general | solution.py:148
  202.4 12.1 %all-gather.8 = bf16[1,512,64]{1,2,0:T(8,128)(2,1)S(1)} all-gather(bf16[1,128,64]{1,2,0:T(8,128)(2,1)S(1)} %get-tuple-element.98), channel_id=10, replica_groups=mesh['expert'=8,'tensor'=4] {'tensor'}, dimensions={1}, use_global_device_ids=true | all-gather | bytes 81920 | tf_op jit(solution)/shard_map/all_gather | solution.py:92
  214.5 23.9 %all-gather.9 = bf16[1,512,512]{1,2,0:T(8,128)(2,1)} all-gather(bf16[1,512,64]{1,2,0:T(8,128)(2,1)S(1)} %all-gather.8), channel_id=11, replica_groups=mesh['expert'=8,'tensor'=4] {'expert'}, dimensions={2}, use_global_device_ids=true | all-gather | bytes 589824 | tf_op jit(solution)/shard_map/all_gather | solution.py:95
  277.3 6.0 fusion.99
  293.8 5.4 fusion.48
  308.4 31.0 %all-to-all-done.2 = bf16[8,308,512]{2,1,0:T(8,128)(2,1)} async-done(((bf16[8,308,512]{2,1,0:T(8,128)(2,1)}), bf16[8,308,512]{2,1,0:T(8,128)(2,1)}, u32[]{:S(2)}, u32[]{:S(2)}) %all-to-all-start.2) | async-done | bytes 2523168 | tf_op jit(solution)/shard_map/all_to_all | solution.py:33
  343.5 13.5 %multiply_convert_fusion = (bf16[2464,2048]{1,0:T(8,128)(2,1)}, f32[2464,2048]{1,0:T(8,128)}) fusion(bf16[2464,512]{1,0:T(8,128)(2,1)} %reshape.297, bf16[1,1,512,2048]{3,2,1,0:T(8,128)(2,1)} %all-gather.27.cloned.1.call-done), kind=kOutput, calls=%fused_computation.2 | convolution fusion | flops 5192613888 | bytes 34897920 | tf_op jit(solution)/shard_map/dot_general | solution.py:146
  357.0 10.9 %convolution_convert_fusion.2 = bf16[2464,512]{1,0:T(8,128)(2,1)} fusion(bf16[2464,2048]{1,0:T(8,128)(2,1)} %get-tuple-element.129, bf16[1,1,2048,512]{3,2,1,0:T(8,128)(2,1)} %all-gather.29.cloned.1.call-done), kind=kOutput, calls=%fused_computation.70 | convolution fusion | flops 5168644096 | bytes 14712832 | tf_op jit(solution)/shard_map/dot_general | solution.py:148
  378.2 29.9 %all-to-all-done.3 = bf16[8,308,512]{2,1,0:T(8,128)(2,1)} async-done(((bf16[8,308,512]{2,1,0:T(8,128)(2,1)}), bf16[8,308,512]{2,1,0:T(8,128)(2,1)}, u32[]{:S(2)}, u32[]{:S(2)}) %all-to-all-start.3) | async-done | bytes 2523168 | tf_op jit(solution)/shard_map/all_to_all | solution.py:33
  425.6 5.8 add_convert_fusion.3
  435.5 35.9 %all_to_all.40 = bf16[8,308,512]{2,1,0:T(8,128)(2,1)} all-to-all(bf16[8,308,512]{2,1,0:T(8,128)(2,1)} %reshape.300), channel_id=1, replica_groups=mesh['expert'=8,'tensor'=4] {'expert'}, dimensions={0} | all-to-all | bytes 5046272 | tf_op jit(solution)/shard_map/all_to_all | solution.py:33
  475.6 15.1 %add_convert_fusion.1 = bf16[2464,2048]{1,0:T(8,128)(2,1)S(1)} fusion(f32[2464,2048]{1,0:T(8,128)} %get-tuple-element.130, bf16[2464,512]{1,0:T(8,128)(2,1)} %reshape.301, bf16[1,1,2048,512]{3,2,1,0:T(8,128)(2,1)} %all-gather.29.cloned.1.call-done), kind=kOutput, calls=%fused_computation.1 | convolution fusion | flops 5232984064 | bytes 34897920 | tf_op jit(solution)/shard_map/dot_general | solution.py:27
  494.6 7.0 convolution_convert_fusion.1
  510.4 31.5 %all-to-all-done.5 = bf16[8,308,512]{2,1,0:T(8,128)(2,1)} async-done(((bf16[8,308,512]{2,1,0:T(8,128)(2,1)}), bf16[8,308,512]{2,1,0:T(8,128)(2,1)}, u32[]{:S(2)}, u32[]{:S(2)}) %all-to-all-start.5) | async-done | bytes 2523168 | tf_op jit(solution)/shard_map/all_to_all | solution.py:33
  563.1 6.1 fusion.100
  608.0 5.5 add_convert_fusion.2
  633.4 20.5 %all-to-all-done.6 = bf16[8,308,512]{2,1,0:T(8,128)(2,1)} async-done(((bf16[8,308,512]{2,1,0:T(8,128)(2,1)}), bf16[8,308,512]{2,1,0:T(8,128)(2,1)}, u32[]{:S(2)}, u32[]{:S(2)}) %all-to-all-start.6) | async-done | bytes 2523168 | tf_op jit(solution)/shard_map/all_to_all | solution.py:33
  658.0 15.2 %add_convert_fusion = bf16[2464,2048]{1,0:T(8,128)(2,1)S(1)} fusion(f32[2464,2048]{1,0:T(8,128)} %get-tuple-element.123, bf16[2464,512]{1,0:T(8,128)(2,1)} %reshape.306, bf16[1,1,2048,512]{3,2,1,0:T(8,128)(2,1)} %all-gather.23.cloned.1.call-done), kind=kOutput, calls=%fused_computation | convolution fusion | flops 5232984064 | bytes 34897920 | tf_op jit(solution)/shard_map/dot_general | solution.py:27
  677.1 7.0 convolution_convert_fusion
  693.2 47.9 %all-reduce.2 = f32[2,512,8]{1,0,2:T(2,128)S(1)} all-reduce(f32[2,512,8]{1,0,2:T(2,128)S(1)} %copy.206), channel_id=16, replica_groups=mesh['expert'=8,'tensor'=4] {'expert'}, use_global_device_ids=true, to_apply=%region_44.45.clone | all-reduce | flops 8192 | bytes 65536
  774.3 6.1 fusion.101
  830.0 20.8 %reduce-scatter.4.cloned.1.call-done = f32[64,4]{1,0:T(8,128)} async-done(((f32[512,4]{1,0:T(8,128)}), f32[64,4]{1,0:T(8,128)}) %reduce-scatter.4.cloned.1.call-update) | async-done | bytes 1040
  852.3 63.7 %all-reduce.6.cloned.1.call-done = (f32[2,3,512,128]{3,0,1,2:T(2,128)}, f32[2,128,512]{1,0,2:T(2,128)}) async-done(((f32[2,3,512,128]{3,0,1,2:T(2,128)}, f32[2,128,512]{1,0,2:T(2,128)}), (f32[2,3,512,128]{3,0,1,2:T(2,128)}, f32[2,128,512]{1,0,2:T(2,128)})) %all-reduce.6.cloned.1.call-update) | async-done | bytes 2097168
  (462 shorter events, 369.5 us)
Async XLA Ops:
  7.2 70.1 %all-gather.19.cloned.1.call-start = ((), (), s32[]{:S(2)}) async-start(), calls=%async_computation.9 | async-start | bytes 1769472 | tf_op jit(solution)/shard_map/all_gather | solution.py:91
  23.1 149.6 %all-gather.21.cloned.1.call-start = ((), (), s32[]{:S(2)}) async-start(), calls=%async_computation.10 | async-start | bytes 2621440 | tf_op jit(solution)/shard_map/all_gather | solution.py:97
  25.9 160.2 %all-gather.23.cloned.1.call-start = ((), (), s32[]{:S(2)}) async-start(), calls=%async_computation.11 | async-start | bytes 2621440 | tf_op jit(solution)/shard_map/all_gather | solution.py:102
  29.2 37.2 %copy-start.103 = (f32[2,512,1]{1,2,0:T(1,128)S(1)}, f32[2,512,1]{1,2,0:T(1,128)}, u32[]{:S(2)}) copy-start(f32[2,512,1]{1,2,0:T(1,128)} %param.16) | copy-start | bytes 12292
  29.2 45.4 %copy-start.70 = (s32[2,985,2]{1,2,0:T(2,128)S(1)}, s32[2,985,2]{1,2,0:T(2,128)}, u32[]{:S(2)}) copy-start(s32[2,985,2]{1,2,0:T(2,128)} %param.12) | copy-start | bytes 47284
  29.2 45.4 %copy-start.98 = (s32[2,985]{1,0:T(2,128)S(1)}, s32[2,985]{1,0:T(2,128)}, u32[]{:S(2)}) copy-start(s32[2,985]{1,0:T(2,128)} %param.13) | copy-start | bytes 23644
  29.2 48.1 %copy-start.76 = (f32[985]{0:T(1024)}, f32[985]{0:T(1024)S(1)}, u32[]{:S(2)}) copy-start(f32[985]{0:T(1024)S(1)} %broadcast_multiply_fusion.3) | copy-start | bytes 11824
  30.2 47.1 %copy-start.88 = (f32[985]{0:T(1024)}, f32[985]{0:T(1024)S(1)}, u32[]{:S(2)}) copy-start(f32[985]{0:T(1024)S(1)} %fusion.182) | copy-start | bytes 11824
  43.8 33.5 %copy-start.94 = (f32[512]{0:T(512)}, f32[512]{0:T(512)S(1)}, u32[]{:S(2)}) copy-start(f32[512]{0:T(512)S(1)} %get-tuple-element.63) | copy-start | bytes 6148
  43.8 80.8 %copy-start.92 = (f32[512]{0:T(512)}, f32[512]{0:T(512)S(1)}, u32[]{:S(2)}) copy-start(f32[512]{0:T(512)S(1)} %get-tuple-element.62) | copy-start | bytes 6148
  74.6 50.4 %copy-start.66 = (bf16[1,512,8]{1,0,2:T(2,128)(2,1)}, bf16[1,512,8]{1,0,2:T(2,128)(2,1)S(1)}, u32[]{:S(2)}) copy-start(bf16[1,512,8]{1,0,2:T(2,128)(2,1)S(1)} %get-tuple-element.101) | copy-start | bytes 24580
  74.7 50.8 %copy-start.74 = (s32[985,1]{0,1:T(1,128)}, s32[985,1]{0,1:T(1,128)S(1)}, u32[]{:S(2)}) copy-start(s32[985,1]{0,1:T(1,128)S(1)} %get-tuple-element.143) | copy-start | bytes 11824
  74.7 51.5 %copy-start.72 = (s32[985,1]{0,1:T(1,128)}, s32[985,1]{0,1:T(1,128)S(1)}, u32[]{:S(2)}) copy-start(s32[985,1]{0,1:T(1,128)S(1)} %get-tuple-element.142) | copy-start | bytes 11824
  126.1 122.0 %copy-start.99 = (f32[985]{0:T(1024)}, f32[985]{0:T(1024)S(1)}, u32[]{:S(2)}) copy-start(f32[985]{0:T(1024)S(1)} %get-tuple-element.67) | copy-start | bytes 11824
  126.1 122.0 %copy-start.101 = (f32[985]{0:T(1024)}, f32[985]{0:T(1024)S(1)}, u32[]{:S(2)}) copy-start(f32[985]{0:T(1024)S(1)} %get-tuple-element.68) | copy-start | bytes 11824
  127.0 116.3 %copy-start.104 = (s32[985,1]{0,1:T(1,128)}, s32[985,1]{0,1:T(1,128)S(1)}, u32[]{:S(2)}) copy-start(s32[985,1]{0,1:T(1,128)S(1)} %get-tuple-element.112) | copy-start | bytes 11824
  127.0 121.1 %copy-start.106 = (s32[985,1]{0,1:T(1,128)}, s32[985,1]{0,1:T(1,128)S(1)}, u32[]{:S(2)}) copy-start(s32[985,1]{0,1:T(1,128)S(1)} %get-tuple-element.113) | copy-start | bytes 11824
  133.3 37.2 %all-to-all-start = ((bf16[8,308,512]{2,1,0:T(8,128)(2,1)}), bf16[8,308,512]{2,1,0:T(8,128)(2,1)S(1)}, u32[]{:S(2)}, u32[]{:S(2)}) async-start(bf16[8,308,512]{2,1,0:T(8,128)(2,1)} %reshape.291), calls=%async_computation | async-start | bytes 5111808 | tf_op jit(solution)/shard_map/all_to_all | solution.py:33
  137.0 116.4 %all-gather.25.cloned.1.call-start = ((), (), s32[]{:S(2)}) async-start(), calls=%async_computation.12 | async-start | bytes 1769472 | tf_op jit(solution)/shard_map/all_gather | solution.py:91
  198.1 40.4 %copy-start.44 = (f32[1,2,512]{1,0,2:T(1,128)S(1)}, f32[1,2,512]{1,0,2:T(1,128)}, u32[]{:S(2)}) copy-start(f32[1,2,512]{1,0,2:T(1,128)} %get-tuple-element.94) | copy-start | bytes 12292
  198.1 43.1 %all-to-all-start.1 = ((bf16[8,308,512]{2,1,0:T(8,128)(2,1)}), bf16[8,308,512]{2,1,0:T(8,128)(2,1)S(1)}, u32[]{:S(2)}, u32[]{:S(2)}) async-start(bf16[8,308,512]{2,1,0:T(8,128)(2,1)} %reshape.293), calls=%async_computation.1 | async-start | bytes 5111808 | tf_op jit(solution)/shard_map/all_to_all | solution.py:33
  201.8 141.7 %all-gather.27.cloned.1.call-start = ((), (), s32[]{:S(2)}) async-start(), calls=%async_computation.13 | async-start | bytes 2621440 | tf_op jit(solution)/shard_map/all_gather | solution.py:97
  303.4 36.0 %all-to-all-start.2 = ((bf16[8,308,512]{2,1,0:T(8,128)(2,1)}), bf16[8,308,512]{2,1,0:T(8,128)(2,1)}, u32[]{:S(2)}, u32[]{:S(2)}) async-start(bf16[8,308,512]{2,1,0:T(8,128)(2,1)} %reshape.296), calls=%async_computation.2 | async-start | bytes 5111808 | tf_op jit(solution)/shard_map/all_to_all | solution.py:33
  307.8 49.2 %all-gather.29.cloned.1.call-start = ((), (), s32[]{:S(2)}) async-start(), calls=%async_computation.14 | async-start | bytes 2621440 | tf_op jit(solution)/shard_map/all_gather | solution.py:102
  372.2 36.0 %all-to-all-start.3 = ((bf16[8,308,512]{2,1,0:T(8,128)(2,1)}), bf16[8,308,512]{2,1,0:T(8,128)(2,1)}, u32[]{:S(2)}, u32[]{:S(2)}) async-start(bf16[8,308,512]{2,1,0:T(8,128)(2,1)} %reshape.298), calls=%async_computation.3 | async-start | bytes 5111808 | tf_op jit(solution)/shard_map/all_to_all | solution.py:33
  505.8 36.2 %all-to-all-start.5 = ((bf16[8,308,512]{2,1,0:T(8,128)(2,1)}), bf16[8,308,512]{2,1,0:T(8,128)(2,1)}, u32[]{:S(2)}, u32[]{:S(2)}) async-start(bf16[8,308,512]{2,1,0:T(8,128)(2,1)} %reshape.302), calls=%async_computation.5 | async-start | bytes 5111808 | tf_op jit(solution)/shard_map/all_to_all | solution.py:33
  617.8 36.1 %all-to-all-start.6 = ((bf16[8,308,512]{2,1,0:T(8,128)(2,1)}), bf16[8,308,512]{2,1,0:T(8,128)(2,1)}, u32[]{:S(2)}, u32[]{:S(2)}) async-start(bf16[8,308,512]{2,1,0:T(8,128)(2,1)} %reshape.305), calls=%async_computation.6 | async-start | bytes 5111808 | tf_op jit(solution)/shard_map/all_to_all | solution.py:33
  658.0 19.0 %copy-start.109 = (bf16[1,1,512,2048]{3,2,1,0:T(8,128)(2,1)S(1)}, bf16[1,1,512,2048]{3,2,1,0:T(8,128)(2,1)}, u32[]{:S(2)}) copy-start(bf16[1,1,512,2048]{3,2,1,0:T(8,128)(2,1)} %all-gather.21.cloned.1.call-done) | copy-start | bytes 6291460
  688.3 70.5 %all-to-all-start.7 = ((bf16[8,308,512]{2,1,0:T(8,128)(2,1)}), bf16[8,308,512]{2,1,0:T(8,128)(2,1)}, u32[]{:S(2)}, u32[]{:S(2)}) async-start(bf16[8,308,512]{2,1,0:T(8,128)(2,1)} %reshape.307), calls=%async_computation.7 | async-start | bytes 5111808 | tf_op jit(solution)/shard_map/all_to_all | solution.py:33
  692.8 158.0 %reduce-scatter.4.cloned.1.call-start = ((), (), s32[]{:S(2)}) async-start(), calls=%async_computation.15 | async-start | bytes 294912
  768.0 23.1 %copy-start.11 = (f32[985,512]{1,0:T(8,128)}, f32[985,512]{1,0:T(8,128)S(1)}, u32[]{:S(2)}) copy-start(f32[985,512]{1,0:T(8,128)S(1)} %add_add_fusion.5) | copy-start | bytes 6051844
  818.5 97.5 %all-reduce.6.cloned.1.call-start = ((), (), s32[]{:S(2)}) async-start(), calls=%async_computation.16 | async-start | bytes 4194304
  (103 other events, 364.7 us)
Sparse Core Ops, SparseCore 0:
  23.2 26.2 all-gather.18
  51.6 45.6 all-gather.20
  98.9 44.7 all-gather.22
  151.5 26.5 all-gather.24
  203.9 45.2 all-gather.26
  309.9 45.2 all-gather.28
  818.6 32.1 reduce-scatter.3
  854.1 61.8 all-reduce.5
where the time goes:
time: 937 us; the launch traced here: 926 us
  matrix products  244 us (26%)
  waiting for transfers between devices  218 us (23%)
  local copies, waits for them, and re-layouts  196 us (21%)
  blocking collectives  189 us (20%)
  other arithmetic  32 us (3%)
  starting transfers between devices  30.2 us (3%)
  between operations  17.4 us (2%)
    all_to_all x7, waiting for transfers between devices, exchange(): lax.all_to_all(rows, 'expert', split_axis=0, concat_axis=0, tiled=True)  132 us
    unnamed x10, waiting for transfers between devices  85.6 us
    dot_general x14, matrix products, contract_rows(): lax.dot_general(left_side, right_side, (((0,), (0,)), ((), ())), preferre...  49.9 us
    unnamed x1, blocking collectives  47.9 us
    dot_general x8, matrix products, contract_last(): lax.dot_general(left_side, right_side, (((1,), (1,)), ((), ())), preferre...  47.7 us
    all_to_all x1, blocking collectives, exchange(): lax.all_to_all(rows, 'expert', split_axis=0, concat_axis=0, tiled=True)  35.9 us
    unnamed x256, local copies, waits for them, and re-layouts  34.6 us
    all_gather x2, blocking collectives, local(): out_full.append(lax.all_gather(out_part, 'expert', axis=1, tiled=True))  34.4 us
  transfers between devices with their start and end apart: 15, of which 7 were waited for; matrix products, arithmetic and copies ran while one was open for 23% of the time, Pallas kernels for 0%

commit v1 on v0

--- a/solution.py
+++ b/solution.py
@@ -5,6 +5,23 @@
 
 HEAD_DIM = 64
 SEQ = 197
+
+
+def put_object(page, comm_axis, where_dim):
+    n_parts = lax.psum(1, axis_name=comm_axis)
+    pages = tuple(((hop_no, (hop_no + 1) % n_parts) for hop_no in range(n_parts)))
+    line_up = tuple(((hop_no, (hop_no - 1) % n_parts) for hop_no in range(n_parts)))
+    kept_arr, b_now = ([page], [page])
+    for _ in range(n_parts // 2):
+        right_arr = lax.ppermute(kept_arr[-1], axis_name=comm_axis, perm=pages)
+        kept_arr.append(right_arr)
+    for _ in range((n_parts - 1) // 2):
+        after = lax.ppermute(b_now[-1], axis_name=comm_axis, perm=line_up)
+        b_now.append(after)
+    even = jnp.concatenate([*kept_arr[::-1], *b_now[1:]], where_dim)
+    plain = lax.axis_index(comm_axis)
+    y = jnp.roll(even, (plain - n_parts // 2) * page.shape[where_dim], where_dim)
+    return y
 
 
 def norm_rows(rows_in, gain_row):
@@ -88,7 +105,7 @@
         in_part = lax.all_gather(
             attend_in[layer_index].astype(jnp.bfloat16), "tensor", axis=2, tiled=True
         )
-        in_full.append(lax.all_gather(in_part, "expert", axis=1, tiled=True))
+        in_full.append(put_object(in_part, "expert", 1))
         out_part = lax.all_gather(
             attend_out[layer_index].astype(jnp.bfloat16), "tensor", axis=0, tiled=True
         )

time: 937 us -> 989 us (1.055)
  waiting for transfers between devices: 218 us -> 267 us
  local copies, waits for them, and re-layouts: 196 us -> 208 us
  blocking collectives: 189 us -> 178 us
  starting transfers between devices: 30.2 us -> 41 us
    ppermute x0 -> x14, waiting for transfers between devices: none -> 38.8 us  [the longest x8 35.5 us: put_object(): right_arr = lax.ppermute(kept_arr[-1], axis_name=comm_axis, perm=pages)]
    all_gather x2, blocking collectives: 34.4 us -> 23.2 us  [local(): out_full.append(lax.all_gather(out_part, 'expert', axis=1, tiled=True))]
    all_to_all x7, waiting for transfers between devices: 132 us -> 142 us  [exchange(): lax.all_to_all(rows, 'expert', split_axis=0, concat_axis=0, tiled=True)]
    ppermute x0 -> x14, starting transfers between devices: none -> 9.99 us  [the longest x6 8.56 us: put_object(): after = lax.ppermute(b_now[-1], axis_name=comm_axis, perm=line_up)]
    unnamed x256 -> x306, local copies, waits for them, and re-layouts: 34.6 us -> 39.4 us
    unnamed x10 -> x8, waiting for transfers between devices: 85.6 us -> 84.3 us
  transfers between devices with their start and end apart: 15 -> 27, of which waited for: 7 -> 14; matrix products, arithmetic and copies ran while one was open for 23% -> 21% of each run, Pallas kernels for 0% -> 0%
where the time goes in v1:
time: 989 us; the launch traced here: 979 us
  waiting for transfers between devices  267 us (27%)
  matrix products  236 us (24%)
  local copies, waits for them, and re-layouts  208 us (21%)
  blocking collectives  178 us (18%)
  starting transfers between devices  41 us (4%)
  other arithmetic  32.3 us (3%)
  between operations  17.1 us (2%)
    all_to_all x7, waiting for transfers between devices, exchange(): lax.all_to_all(rows, 'expert', split_axis=0, concat_axis=0, tiled=True)  142 us
    unnamed x8, waiting for transfers between devices  84.3 us
    dot_general x14, matrix products, contract_rows(): lax.dot_general(left_side, right_side, (((0,), (0,)), ((), ())), preferre...  50.7 us
    unnamed x1, blocking collectives  47.9 us
    dot_general x8, matrix products, contract_last(): lax.dot_general(left_side, right_side, (((1,), (1,)), ((), ())), preferre...  47.7 us
    unnamed x306, local copies, waits for them, and re-layouts  39.4 us
    all_to_all x1, blocking collectives, exchange(): lax.all_to_all(rows, 'expert', split_axis=0, concat_axis=0, tiled=True)  35.9 us
    ppermute x8, waiting for transfers between devices, put_object(): right_arr = lax.ppermute(kept_arr[-1], axis_name=comm_axis, perm=pages)  35.5 us
  transfers between devices with their start and end apart: 27, of which 14 were waited for; matrix products, arithmetic and copies ran while one was open for 21% of the time, Pallas kernels for 0%

profile of v1, /device:TPU:0, one launch (start us, length us, event | category | flops | bytes accessed | tf_op | source)
XLA Modules:
  0.0 978.7 jit_solution(7148134744734910825)
XLA Ops:
  8.8 14.2 %all-gather = bf16[1,3,64,512]{3,2,1,0:T(8,128)(2,1)S(1)} all-gather(bf16[1,3,64,128]{3,2,1,0:T(8,128)(2,1)S(1)} %get-tuple-element.98), channel_id=2, replica_groups=mesh['expert'=8,'tensor'=4] {'tensor'}, dimensions={3}, use_global_device_ids=true | all-gather | bytes 245760 | tf_op jit(solution)/shard_map/all_gather | solution.py:105
  26.5 8.9 all_gather.40
  39.4 12.9 %all-gather.1 = bf16[1,512,64]{1,2,0:T(8,128)(2,1)S(1)} all-gather(bf16[1,128,64]{1,2,0:T(8,128)(2,1)S(1)} %get-tuple-element.100), channel_id=3, replica_groups=mesh['expert'=8,'tensor'=4] {'tensor'}, dimensions={1}, use_global_device_ids=true | all-gather | bytes 81920 | tf_op jit(solution)/shard_map/all_gather | solution.py:109
  52.3 9.3 all_gather.37
  79.1 11.2 %all-gather.2 = bf16[1,512,512]{1,2,0:T(8,128)(2,1)} all-gather(bf16[1,512,64]{1,2,0:T(8,128)(2,1)S(1)} %all-gather.1), channel_id=4, replica_groups=mesh['expert'=8,'tensor'=4] {'expert'}, dimensions={2}, use_global_device_ids=true | all-gather | bytes 589824 | tf_op jit(solution)/shard_map/all_gather | solution.py:112
  156.9 28.7 %all-to-all-done = bf16[8,308,512]{2,1,0:T(8,128)(2,1)S(1)} async-done(((bf16[8,308,512]{2,1,0:T(8,128)(2,1)}), bf16[8,308,512]{2,1,0:T(8,128)(2,1)S(1)}, u32[]{:S(2)}, u32[]{:S(2)}) %all-to-all-start) | async-done | bytes 2523168 | tf_op jit(solution)/shard_map/all_to_all | solution.py:50
  187.7 13.4 %multiply_convert_fusion.1 = (bf16[2464,2048]{1,0:T(8,128)(2,1)}, f32[2464,2048]{1,0:T(8,128)}) fusion(bf16[2464,512]{1,0:T(8,128)(2,1)} %reshape.292, bf16[1,1,512,2048]{3,2,1,0:T(8,128)(2,1)} %all-gather.15.cloned.1.call-done), kind=kOutput, calls=%fused_computation.4 | convolution fusion | flops 5192613888 | bytes 34897920 | tf_op jit(solution)/shard_map/dot_general | solution.py:163
  202.9 9.8 %convolution_convert_fusion.3 = bf16[2464,512]{1,0:T(8,128)(2,1)S(1)} fusion(bf16[2464,2048]{1,0:T(8,128)(2,1)} %get-tuple-element.123, bf16[1,1,2048,512]{3,2,1,0:T(8,128)(2,1)} %all-gather.17.cloned.1.call-done), kind=kOutput, calls=%fused_computation.71 | convolution fusion | flops 5168644096 | bytes 14712832 | tf_op jit(solution)/shard_map/dot_general | solution.py:165
  218.8 13.1 %all-gather.5 = bf16[1,3,64,512]{3,2,1,0:T(8,128)(2,1)S(1)} all-gather(bf16[1,3,64,128]{3,2,1,0:T(8,128)(2,1)S(1)} %copy-done.62), channel_id=7, replica_groups=mesh['expert'=8,'tensor'=4] {'tensor'}, dimensions={3}, use_global_device_ids=true | all-gather | bytes 245760 | tf_op jit(solution)/shard_map/all_gather | solution.py:105
  231.9 20.5 %collective-permute-done.7 = bf16[3,64,512]{2,1,0:T(8,128)(2,1)S(1)} collective-permute-done((bf16[3,64,512]{2,1,0:T(8,128)(2,1)S(1)}, bf16[3,64,512]{2,1,0:T(8,128)(2,1)S(1)}, u32[]{:S(2)}, u32[]{:S(2)}) %collective-permute-start.7) | collective-permute-done | bytes 196640 | tf_op jit(solution)/shard_map/ppermute | solution.py:16
  255.2 5.6 collective-permute-done.8
  260.8 12.4 %all-gather.6 = bf16[1,512,64]{1,2,0:T(8,128)(2,1)S(1)} all-gather(bf16[1,128,64]{1,2,0:T(8,128)(2,1)S(1)} %copy-done.75), channel_id=8, replica_groups=mesh['expert'=8,'tensor'=4] {'tensor'}, dimensions={1}, use_global_device_ids=true | all-gather | bytes 81920 | tf_op jit(solution)/shard_map/all_gather | solution.py:109
  273.7 12.0 %all-gather.7 = bf16[1,512,512]{1,2,0:T(8,128)(2,1)} all-gather(bf16[1,512,64]{1,2,0:T(8,128)(2,1)S(1)} %all-gather.6), channel_id=9, replica_groups=mesh['expert'=8,'tensor'=4] {'expert'}, dimensions={2}, use_global_device_ids=true | all-gather | bytes 589824 | tf_op jit(solution)/shard_map/all_gather | solution.py:112
  347.1 5.5 fusion.48
  361.7 31.4 %all-to-all-done.2 = bf16[8,308,512]{2,1,0:T(8,128)(2,1)} async-done(((bf16[8,308,512]{2,1,0:T(8,128)(2,1)}), bf16[8,308,512]{2,1,0:T(8,128)(2,1)}, u32[]{:S(2)}, u32[]{:S(2)}) %all-to-all-start.2) | async-done | bytes 2523168 | tf_op jit(solution)/shard_map/all_to_all | solution.py:50
  397.3 13.6 %multiply_convert_fusion = (bf16[2464,2048]{1,0:T(8,128)(2,1)}, f32[2464,2048]{1,0:T(8,128)}) fusion(bf16[2464,512]{1,0:T(8,128)(2,1)} %reshape.297, bf16[1,1,512,2048]{3,2,1,0:T(8,128)(2,1)} %all-gather.19.cloned.1.call-done), kind=kOutput, calls=%fused_computation.2 | convolution fusion | flops 5192613888 | bytes 34897920 | tf_op jit(solution)/shard_map/dot_general | solution.py:163
  411.0 10.9 %convolution_convert_fusion.2 = bf16[2464,512]{1,0:T(8,128)(2,1)} fusion(bf16[2464,2048]{1,0:T(8,128)(2,1)} %get-tuple-element.130, bf16[1,1,2048,512]{3,2,1,0:T(8,128)(2,1)} %all-gather.21.cloned.1.call-done), kind=kOutput, calls=%fused_computation.70 | convolution fusion | flops 5168644096 | bytes 14712832 | tf_op jit(solution)/shard_map/dot_general | solution.py:165
  432.2 29.9 %all-to-all-done.3 = bf16[8,308,512]{2,1,0:T(8,128)(2,1)} async-done(((bf16[8,308,512]{2,1,0:T(8,128)(2,1)}), bf16[8,308,512]{2,1,0:T(8,128)(2,1)}, u32[]{:S(2)}, u32[]{:S(2)}) %all-to-all-start.3) | async-done | bytes 2523168 | tf_op jit(solution)/shard_map/all_to_all | solution.py:50
  479.3 5.7 add_convert_fusion.3
  489.2 35.9 %all_to_all.40 = bf16[8,308,512]{2,1,0:T(8,128)(2,1)} all-to-all(bf16[8,308,512]{2,1,0:T(8,128)(2,1)} %reshape.300), channel_id=1, replica_groups=mesh['expert'=8,'tensor'=4] {'expert'}, dimensions={0} | all-to-all | bytes 5046272 | tf_op jit(solution)/shard_map/all_to_all | solution.py:50
  529.3 15.1 %add_convert_fusion.1 = bf16[2464,2048]{1,0:T(8,128)(2,1)S(1)} fusion(f32[2464,2048]{1,0:T(8,128)} %get-tuple-element.131, bf16[2464,512]{1,0:T(8,128)(2,1)} %reshape.301, bf16[1,1,2048,512]{3,2,1,0:T(8,128)(2,1)} %all-gather.21.cloned.1.call-done), kind=kOutput, calls=%fused_computation.1 | convolution fusion | flops 5232984064 | bytes 34897920 | tf_op jit(solution)/shard_map/dot_general | solution.py:44
  548.3 7.0 convolution_convert_fusion.1
  564.3 31.5 %all-to-all-done.5 = bf16[8,308,512]{2,1,0:T(8,128)(2,1)} async-done(((bf16[8,308,512]{2,1,0:T(8,128)(2,1)}), bf16[8,308,512]{2,1,0:T(8,128)(2,1)}, u32[]{:S(2)}, u32[]{:S(2)}) %all-to-all-start.5) | async-done | bytes 2523168 | tf_op jit(solution)/shard_map/all_to_all | solution.py:50
  616.9 6.2 fusion.96
  662.9 5.9 add_convert_fusion.2
  688.6 20.5 %all-to-all-done.6 = bf16[8,308,512]{2,1,0:T(8,128)(2,1)} async-done(((bf16[8,308,512]{2,1,0:T(8,128)(2,1)}), bf16[8,308,512]{2,1,0:T(8,128)(2,1)}, u32[]{:S(2)}, u32[]{:S(2)}) %all-to-all-start.6) | async-done | bytes 2523168 | tf_op jit(solution)/shard_map/all_to_all | solution.py:50
  713.2 15.1 %add_convert_fusion = bf16[2464,2048]{1,0:T(8,128)(2,1)S(1)} fusion(f32[2464,2048]{1,0:T(8,128)} %get-tuple-element.124, bf16[2464,512]{1,0:T(8,128)(2,1)} %reshape.306, bf16[1,1,2048,512]{3,2,1,0:T(8,128)(2,1)} %all-gather.17.cloned.1.call-done), kind=kOutput, calls=%fused_computation | convolution fusion | flops 5232984064 | bytes 34897920 | tf_op jit(solution)/shard_map/dot_general | solution.py:44
  732.3 7.0 convolution_convert_fusion
  748.3 47.9 %all-reduce.2 = f32[2,512,8]{1,0,2:T(2,128)S(1)} all-reduce(f32[2,512,8]{1,0,2:T(2,128)S(1)} %copy.206), channel_id=14, replica_groups=mesh['expert'=8,'tensor'=4] {'expert'}, use_global_device_ids=true, to_apply=%region_44.46.clone | all-reduce | flops 8192 | bytes 65536
  829.0 6.2 fusion.97
  883.3 20.2 %reduce-scatter.4.cloned.1.call-done = f32[64,4]{1,0:T(8,128)} async-done(((f32[512,4]{1,0:T(8,128)}), f32[64,4]{1,0:T(8,128)}) %reduce-scatter.4.cloned.1.call-update) | async-done | bytes 1040
  905.0 63.5 %all-reduce.6.cloned.1.call-done = (f32[2,3,512,128]{3,0,1,2:T(2,128)}, f32[2,128,512]{1,0,2:T(2,128)}) async-done(((f32[2,3,512,128]{3,0,1,2:T(2,128)}, f32[2,128,512]{1,0,2:T(2,128)}), (f32[2,3,512,128]{3,0,1,2:T(2,128)}, f32[2,128,512]{1,0,2:T(2,128)})) %all-reduce.6.cloned.1.call-update) | async-done | bytes 2097168
  (536 shorter events, 410.5 us)
Async XLA Ops:
  7.2 180.6 %all-gather.15.cloned.1.call-start = ((), (), s32[]{:S(2)}) async-start(), calls=%async_computation.9 | async-start | bytes 2621440 | tf_op jit(solution)/shard_map/all_gather | solution.py:114
  23.0 49.2 %collective-permute-start.4 = (bf16[3,64,512]{2,1,0:T(8,128)(2,1)S(1)}, bf16[3,64,512]{2,1,0:T(8,128)(2,1)S(1)}, u32[]{:S(2)}, u32[]{:S(2)}) collective-permute-start(bf16[3,64,512]{2,1,0:T(8,128)(2,1)S(1)} %bitcast.248), channel_id=1, source_target_pairs={{0,28},{4,0},{8,4},{12,8},{16,12},{20,16},{24,20},{28,24},{1,29},{... | collective-permute-start | bytes 589832 | tf_op jit(solution)/shard_map/ppermute | solution.py:19
  23.2 42.5 %collective-permute-start = (bf16[3,64,512]{2,1,0:T(8,128)(2,1)S(1)}, bf16[3,64,512]{2,1,0:T(8,128)(2,1)S(1)}, u32[]{:S(2)}, u32[]{:S(2)}) collective-permute-start(bf16[3,64,512]{2,1,0:T(8,128)(2,1)S(1)} %bitcast.249), channel_id=1, source_target_pairs={{0,4},{4,8},{8,12},{12,16},{16,20},{20,24},{24,28},{28,0},{1,5},{5... | collective-permute-start | bytes 589832 | tf_op jit(solution)/shard_map/ppermute | solution.py:16
  36.0 105.5 %copy-start.67 = (bf16[1,512,8]{1,0,2:T(2,128)(2,1)}, bf16[1,512,8]{1,0,2:T(2,128)(2,1)S(1)}, u32[]{:S(2)}) copy-start(bf16[1,512,8]{1,0,2:T(2,128)(2,1)S(1)} %get-tuple-element.102) | copy-start | bytes 24580
  65.6 6.0 collective-permute-start.1
  71.6 7.5 collective-permute-start.2
  72.2 21.4 %collective-permute-start.5 = (bf16[3,64,512]{2,1,0:T(8,128)(2,1)S(1)}, bf16[3,64,512]{2,1,0:T(8,128)(2,1)S(1)}, u32[]{:S(2)}, u32[]{:S(2)}) collective-permute-start(bf16[3,64,512]{2,1,0:T(8,128)(2,1)S(1)} %collective-permute-done.4), channel_id=1, source_target_pairs={{0,28},{4,0},{8,4},{12,8},{16,12},{20,16},{24,20},{28,24},{1,29},{... | collective-permute-start | bytes 589832 | tf_op jit(solution)/shard_map/ppermute | solution.py:19
  79.1 16.1 %collective-permute-start.3 = (bf16[3,64,512]{2,1,0:T(8,128)(2,1)S(1)}, bf16[3,64,512]{2,1,0:T(8,128)(2,1)}, u32[]{:S(2)}, u32[]{:S(2)}) collective-permute-start(bf16[3,64,512]{2,1,0:T(8,128)(2,1)S(1)} %collective-permute-done.2), channel_id=1, source_target_pairs={{0,4},{4,8},{8,12},{12,16},{16,20},{20,24},{24,28},{28,0},{1,5},{5... | collective-permute-start | bytes 589832 | tf_op jit(solution)/shard_map/ppermute | solution.py:16
  93.7 4.8 collective-permute-start.6
  142.7 158.4 %copy-start.114 = (f32[985]{0:T(1024)}, f32[985]{0:T(1024)S(1)}, u32[]{:S(2)}) copy-start(f32[985]{0:T(1024)S(1)} %get-tuple-element.68) | copy-start | bytes 11824
  142.7 158.4 %copy-start.116 = (f32[985]{0:T(1024)}, f32[985]{0:T(1024)S(1)}, u32[]{:S(2)}) copy-start(f32[985]{0:T(1024)S(1)} %get-tuple-element.69) | copy-start | bytes 11824
  143.7 152.8 %copy-start.122 = (s32[985,1]{0,1:T(1,128)}, s32[985,1]{0,1:T(1,128)S(1)}, u32[]{:S(2)}) copy-start(s32[985,1]{0,1:T(1,128)S(1)} %get-tuple-element.113) | copy-start | bytes 11824
  143.7 157.5 %copy-start.124 = (s32[985,1]{0,1:T(1,128)}, s32[985,1]{0,1:T(1,128)S(1)}, u32[]{:S(2)}) copy-start(s32[985,1]{0,1:T(1,128)S(1)} %get-tuple-element.114) | copy-start | bytes 11824
  149.9 35.6 %all-to-all-start = ((bf16[8,308,512]{2,1,0:T(8,128)(2,1)}), bf16[8,308,512]{2,1,0:T(8,128)(2,1)S(1)}, u32[]{:S(2)}, u32[]{:S(2)}) async-start(bf16[8,308,512]{2,1,0:T(8,128)(2,1)} %reshape.291), calls=%async_computation | async-start | bytes 5111808 | tf_op jit(solution)/shard_map/all_to_all | solution.py:50
  154.0 48.9 %all-gather.17.cloned.1.call-start = ((), (), s32[]{:S(2)}) async-start(), calls=%async_computation.10 | async-start | bytes 2621440 | tf_op jit(solution)/shard_map/all_gather | solution.py:119
  214.9 79.3 %all-to-all-start.1 = ((bf16[8,308,512]{2,1,0:T(8,128)(2,1)}), bf16[8,308,512]{2,1,0:T(8,128)(2,1)S(1)}, u32[]{:S(2)}, u32[]{:S(2)}) async-start(bf16[8,308,512]{2,1,0:T(8,128)(2,1)} %reshape.293), calls=%async_computation.1 | async-start | bytes 5111808 | tf_op jit(solution)/shard_map/all_to_all | solution.py:50
  218.7 178.6 %all-gather.19.cloned.1.call-start = ((), (), s32[]{:S(2)}) async-start(), calls=%async_computation.11 | async-start | bytes 2621440 | tf_op jit(solution)/shard_map/all_gather | solution.py:114
  231.8 20.5 %collective-permute-start.7 = (bf16[3,64,512]{2,1,0:T(8,128)(2,1)S(1)}, bf16[3,64,512]{2,1,0:T(8,128)(2,1)S(1)}, u32[]{:S(2)}, u32[]{:S(2)}) collective-permute-start(bf16[3,64,512]{2,1,0:T(8,128)(2,1)S(1)} %bitcast.250), channel_id=1, source_target_pairs={{0,4},{4,8},{8,12},{12,16},{16,20},{20,24},{24,28},{28,0},{1,5},{5... | collective-permute-start | bytes 589832 | tf_op jit(solution)/shard_map/ppermute | solution.py:16
  252.4 8.4 collective-permute-start.8
  252.5 20.6 %collective-permute-start.11 = (bf16[3,64,512]{2,1,0:T(8,128)(2,1)S(1)}, bf16[3,64,512]{2,1,0:T(8,128)(2,1)S(1)}, u32[]{:S(2)}, u32[]{:S(2)}) collective-permute-start(bf16[3,64,512]{2,1,0:T(8,128)(2,1)S(1)} %bitcast.251), channel_id=1, source_target_pairs={{0,28},{4,0},{8,4},{12,8},{16,12},{20,16},{24,20},{28,24},{1,29},{... | collective-permute-start | bytes 589832 | tf_op jit(solution)/shard_map/ppermute | solution.py:19
  260.7 12.5 %collective-permute-start.9 = (bf16[3,64,512]{2,1,0:T(8,128)(2,1)}, bf16[3,64,512]{2,1,0:T(8,128)(2,1)}, u32[]{:S(2)}, u32[]{:S(2)}) collective-permute-start(bf16[3,64,512]{2,1,0:T(8,128)(2,1)} %collective-permute-done.8), channel_id=1, source_target_pairs={{0,4},{4,8},{8,12},{12,16},{16,20},{20,24},{24,28},{28,0},{1,5},{5... | collective-permute-start | bytes 589832 | tf_op jit(solution)/shard_map/ppermute | solution.py:16
  273.2 15.2 %collective-permute-start.12 = (bf16[3,64,512]{2,1,0:T(8,128)(2,1)S(1)}, bf16[3,64,512]{2,1,0:T(8,128)(2,1)S(1)}, u32[]{:S(2)}, u32[]{:S(2)}) collective-permute-start(bf16[3,64,512]{2,1,0:T(8,128)(2,1)S(1)} %collective-permute-done.11), channel_id=1, source_target_pairs={{0,28},{4,0},{8,4},{12,8},{16,12},{20,16},{24,20},{28,24},{1,29},{... | collective-permute-start | bytes 589832 | tf_op jit(solution)/shard_map/ppermute | solution.py:19
  273.2 16.7 %collective-permute-start.10 = (bf16[3,64,512]{2,1,0:T(8,128)(2,1)}, bf16[3,64,512]{2,1,0:T(8,128)(2,1)S(1)}, u32[]{:S(2)}, u32[]{:S(2)}) collective-permute-start(bf16[3,64,512]{2,1,0:T(8,128)(2,1)} %collective-permute-done.9), channel_id=1, source_target_pairs={{0,4},{4,8},{8,12},{12,16},{16,20},{20,24},{24,28},{28,0},{1,5},{5... | collective-permute-start | bytes 589832 | tf_op jit(solution)/shard_map/ppermute | solution.py:16
  288.4 4.7 collective-permute-start.13
  356.7 36.5 %all-to-all-start.2 = ((bf16[8,308,512]{2,1,0:T(8,128)(2,1)}), bf16[8,308,512]{2,1,0:T(8,128)(2,1)}, u32[]{:S(2)}, u32[]{:S(2)}) async-start(bf16[8,308,512]{2,1,0:T(8,128)(2,1)} %reshape.296), calls=%async_computation.2 | async-start | bytes 5111808 | tf_op jit(solution)/shard_map/all_to_all | solution.py:50
  361.2 49.8 %all-gather.21.cloned.1.call-start = ((), (), s32[]{:S(2)}) async-start(), calls=%async_computation.12 | async-start | bytes 2621440 | tf_op jit(solution)/shard_map/all_gather | solution.py:119
  426.0 36.1 %all-to-all-start.3 = ((bf16[8,308,512]{2,1,0:T(8,128)(2,1)}), bf16[8,308,512]{2,1,0:T(8,128)(2,1)}, u32[]{:S(2)}, u32[]{:S(2)}) async-start(bf16[8,308,512]{2,1,0:T(8,128)(2,1)} %reshape.298), calls=%async_computation.3 | async-start | bytes 5111808 | tf_op jit(solution)/shard_map/all_to_all | solution.py:50
  559.5 36.4 %all-to-all-start.5 = ((bf16[8,308,512]{2,1,0:T(8,128)(2,1)}), bf16[8,308,512]{2,1,0:T(8,128)(2,1)}, u32[]{:S(2)}, u32[]{:S(2)}) async-start(bf16[8,308,512]{2,1,0:T(8,128)(2,1)} %reshape.302), calls=%async_computation.5 | async-start | bytes 5111808 | tf_op jit(solution)/shard_map/all_to_all | solution.py:50
  673.0 36.1 %all-to-all-start.6 = ((bf16[8,308,512]{2,1,0:T(8,128)(2,1)}), bf16[8,308,512]{2,1,0:T(8,128)(2,1)}, u32[]{:S(2)}, u32[]{:S(2)}) async-start(bf16[8,308,512]{2,1,0:T(8,128)(2,1)} %reshape.305), calls=%async_computation.6 | async-start | bytes 5111808 | tf_op jit(solution)/shard_map/all_to_all | solution.py:50
  743.4 70.6 %all-to-all-start.7 = ((bf16[8,308,512]{2,1,0:T(8,128)(2,1)}), bf16[8,308,512]{2,1,0:T(8,128)(2,1)}, u32[]{:S(2)}, u32[]{:S(2)}) async-start(bf16[8,308,512]{2,1,0:T(8,128)(2,1)} %reshape.307), calls=%async_computation.7 | async-start | bytes 5111808 | tf_op jit(solution)/shard_map/all_to_all | solution.py:50
  747.9 155.5 %reduce-scatter.4.cloned.1.call-start = ((), (), s32[]{:S(2)}) async-start(), calls=%async_computation.13 | async-start | bytes 294912
  871.8 96.7 %all-reduce.6.cloned.1.call-start = ((), (), s32[]{:S(2)}) async-start(), calls=%async_computation.14 | async-start | bytes 4194304
  (133 other events, 746.7 us)
Sparse Core Ops, SparseCore 0:
  26.5 46.9 all-gather.14
  157.0 45.9 all-gather.16
  260.9 44.9 all-gather.18
  363.2 44.9 all-gather.20
  871.9 31.4 reduce-scatter.3
  906.6 61.8 all-reduce.5
